TPU v7x, 256 devices: a whole 4x4x8 slice. The times are simulated.
256 devices in a mesh: sub: 64 (over z, y, core), rhs: 4 (over x).
Axes of the slice: x: 4, y: 4, z: 8, core: 2. Of those that a mesh axis runs over, the one named last changes fastest.
Arguments:
- stiffness: float32 [3072, 4, 9216], P('sub'), may hold values from -1 to 2, as said below
- precond: float32 [3072, 9216], P('sub'), may hold values from -0.625 to 0.625
- rhs_vec: float32 [8, 294912], P('rhs', 'sub'), may hold values from -50 to 50
- cotangent: float32 [8, 294912], P('rhs', 'sub'), may hold values from -6 to 6
- col_index: int32 [3072, 4], P('sub'), may hold values from 0 to 59, as said below
- send_rows: int32 [64, 12], P('sub'), may hold values from 0 to 47, as said below
- counts: int32 [64], P('sub'), may hold values from 12 to 48, as said below
Outputs:
- solution: float32 [8, 294912], P('rhs', 'sub')
- grad_precond: float32 [3072, 9216], P('sub')
Inputs may be any that keep to these rules, and one draw needn't show every extreme that they name: `counts`: at least one subdomain has 48 live block rows. `send_rows`: for subdomain s, entries 0 to 5 are distinct live rows below counts[s] // 2 in increasing order, the first of them 0; entries 6 to 11 are distinct live rows from counts[s] // 2 on in increasing order, the last of them counts[s] - 1. Interface row j of the first group of subdomain s is coupled with interface row j of the second group of subdomain s - 1. `col_index`: index 6 + n is block n of the subdomain; indices below 6 and from 54 on are the blocks received from the previous and the next subdomain. Slot 0 of row n is 6 + n. A slot other than slot 0 that names 6 + n holds a zero block; rows that are not live hold only slot 0's block. `stiffness`: the operator A is symmetric and positive definite.
All inputs are finite; a program needn't handle non-finite values.
Results may differ from a plain program's by a relative error of at most 0.0003.
Values sent between devices are 32-bit elements; how exact they have to be, the bound alone decides.
A program may use at most 128 MiB of HBM per device.

v0:
```python
import jax
import jax.numpy as jnp
from jax import lax
from jax.sharding import PartitionSpec as P

BS = 96
K = 4
NBLK = 48
IF = 6
ITERS = 4
highest = lax.Precision.HIGHEST


def with_halo(array, sides, width):
    for axis, dim in sides:
        size, length = (lax.axis_size(axis), array.shape[dim])
        up = [(i, (i + 1) % size) for i in range(size - 1)]
        down = [(j, i) for i, j in up]
        last = lax.slice_in_dim(array, length - width, length, axis=dim)
        initial = lax.slice_in_dim(array, 0, width, axis=dim)
        before = lax.ppermute(last, axis, up)
        after = lax.ppermute(initial, axis, down)
        array = jnp.concatenate([before, array, after], axis=dim)
    return array


def local_dot(first_vec, second_vec):
    return jnp.sum(first_vec * second_vec, axis=(1, 2))


def widen(scalars):
    return scalars[:, None, None]


def precond_apply(weights, vector):
    projected = jnp.einsum("nab,rnb->rna", weights, vector, precision=highest)
    return (projected, vector + jnp.einsum("nab,rna->rnb", weights, projected, precision=highest))


def block_product(blocks, gathered):
    return jnp.einsum("nkab,rnkb->rna", blocks, gathered, precision=highest)


def stiff_apply(vector, blocks, columns, sending):
    outgoing = jnp.take(vector, sending, axis=1)
    framed = with_halo(outgoing, (("sub", 1),), IF)
    extended = jnp.concatenate([framed[:, :IF], vector, framed[:, 3 * IF :]], axis=1)
    return block_product(blocks, jnp.take(extended, columns, axis=1))


def norm_sum(first_vec, second_vec):
    return lax.psum(local_dot(first_vec, second_vec), "sub")


def grad_term(projected, zeta_bar, weight_zeta, resid_vec):
    first_part = jnp.einsum("rna,rnb->nab", projected, zeta_bar, precision=highest)
    return first_part + jnp.einsum("rna,rnb->nab", weight_zeta, resid_vec, precision=highest)


def shards(stiffness, precond, rhs_vec, cotangent, col_index, send_rows, counts):
    rhs_all, cot_all = (rhs_vec, cotangent)
    local_rhs = rhs_all.shape[0]
    blocks = stiffness.reshape(NBLK, K, BS, BS)
    weights = precond.reshape(NBLK, BS, BS)
    live_count = counts[0]
    sending = send_rows[0]
    live_mask = (jnp.arange(NBLK) < live_count).astype(jnp.float32)
    source = rhs_all.reshape(local_rhs, NBLK, BS) * live_mask[None, :, None]
    target = cot_all.reshape(local_rhs, NBLK, BS)
    residual = source
    first_proj, precon = precond_apply(weights, residual)
    first_res = residual
    direction = precon
    norm_now = norm_sum(residual, precon)
    solution = jnp.zeros_like(source)
    history = []
    for iteration in range(ITERS):
        applied = stiff_apply(direction, blocks, col_index, sending)
        curvature = lax.psum(local_dot(direction, applied), "sub")
        step_len = norm_now / curvature
        solution = solution + widen(step_len) * direction
        residual = residual - widen(step_len) * applied
        record = [direction, applied, step_len, curvature, norm_now]
        if iteration + 1 < ITERS:
            projected, precon = precond_apply(weights, residual)
            norm_next = norm_sum(residual, precon)
            ratio = norm_next / norm_now
            record = record + [residual, precon, projected, norm_next, ratio]
            direction = precon + widen(ratio) * direction
            norm_now = norm_next
        history.append(record)
    dir_bar = jnp.zeros_like(source)
    res_bar = jnp.zeros_like(source)
    norm_bar = jnp.zeros((local_rhs,), jnp.float32)
    grad_sum = jnp.zeros((NBLK, BS, BS), jnp.float32)
    for iteration in reversed(range(ITERS)):
        direction, applied, step_len, curvature, norm_now = history[iteration][:5]
        if iteration + 1 < ITERS:
            resid_next, precon, projected, norm_next, ratio = history[iteration][5:]
            ratio_bar, cot_dir = lax.psum(
                (local_dot(dir_bar, direction), local_dot(target, direction)), "sub"
            )
            norm_full = norm_bar + ratio_bar / norm_now
            zeta_bar = dir_bar + widen(norm_full) * resid_next
            weight_zeta, mapped = precond_apply(weights, zeta_bar)
            res_bar = res_bar + widen(norm_full) * precon + mapped
            res_image = lax.psum(local_dot(res_bar, applied), "sub")
            grad_sum = grad_sum + grad_term(projected, zeta_bar, weight_zeta, resid_next)
            dir_new = widen(ratio) * dir_bar
            norm_new = -ratio_bar * norm_next / (norm_now * norm_now)
        else:
            cot_dir = lax.psum(local_dot(target, direction), "sub")
            res_image = jnp.zeros_like(cot_dir)
            dir_new = jnp.zeros_like(source)
            norm_new = jnp.zeros_like(cot_dir)
        step_bar = cot_dir - res_image
        curv_bar = -step_bar * step_len / curvature
        dir_new = dir_new + widen(step_len) * target + widen(curv_bar) * applied
        image_bar = widen(curv_bar) * direction - widen(step_len) * res_bar
        dir_bar = dir_new + stiff_apply(image_bar, blocks, col_index, sending)
        norm_bar = norm_new + step_bar / curvature
    zeta_bar = dir_bar + widen(norm_bar) * first_res
    weight_zeta = jnp.einsum("nab,rnb->rna", weights, zeta_bar, precision=highest)
    grad_sum = grad_sum + grad_term(first_proj, zeta_bar, weight_zeta, first_res)
    grad_sum = lax.psum(grad_sum, "rhs")
    flat_solution = solution.reshape(local_rhs, NBLK * BS)
    return (flat_solution, grad_sum.reshape(NBLK, BS * BS))


def solution(mesh):
    in_specs = (
        P("sub", None, None),
        P("sub", None),
        P("rhs", "sub"),
        P("rhs", "sub"),
        P("sub", None),
        P("sub", None),
        P("sub"),
    )
    out_specs = (P("rhs", "sub"), P("sub", None))
    return jax.shard_map(shards, mesh=mesh, in_specs=in_specs, out_specs=out_specs, check_vma=False)
```

profile of v0, /device:TPU:1, one launch (start us, length us, event | category | flops | bytes accessed | tf_op | source)
XLA Modules:
  0.0 1994.4 jit_solution(11728397006781931206)
XLA Ops:
  18.9 4.6 collective-permute-start
  25.8 10.6 reshape.54
  37.3 10.5 multiply_reduce_fusion.16
  47.8 127.8 %all-reduce.4 = (f32[2]{0:T(128)S(1)}, f32[2]{0:T(128)S(1)}) all-reduce(f32[2]{0:T(128)S(1)} %get-tuple-element.10, f32[2]{0:T(128)S(1)} %get-tuple-element.9), channel_id=1, replica_groups=mesh['sub'=64,'rhs'=4] {'sub'}, use_global_device_ids=true, to_apply=%region_1.0 | all-reduce | flops 4 | bytes 32 | tf_op jit(solution)/shard_map/psum | solution.py:52
  181.7 127.4 %psum.135 = f32[2]{0:T(128)S(1)} all-reduce(f32[2]{0:T(128)S(1)} %get-tuple-element.44), channel_id=1, replica_groups=mesh['sub'=64,'rhs'=4] {'sub'}, use_global_device_ids=true, to_apply=%region_5.8 | all-reduce | flops 2 | bytes 16 | tf_op jit(solution)/shard_map/psum | solution.py:52
  317.7 10.5 multiply_reduce_fusion.14
  328.2 122.2 %psum.136 = f32[2]{0:T(128)S(1)} all-reduce(f32[2]{0:T(128)S(1)} %get-tuple-element.46), channel_id=1, replica_groups=mesh['sub'=64,'rhs'=4] {'sub'}, use_global_device_ids=true, to_apply=%region_7.10 | all-reduce | flops 2 | bytes 16 | tf_op jit(solution)/shard_map/psum | solution.py:79
  456.5 125.9 %psum.137 = f32[2]{0:T(128)S(1)} all-reduce(f32[2]{0:T(128)S(1)} %get-tuple-element.48), channel_id=1, replica_groups=mesh['sub'=64,'rhs'=4] {'sub'}, use_global_device_ids=true, to_apply=%region_9.12 | all-reduce | flops 2 | bytes 16 | tf_op jit(solution)/shard_map/psum | solution.py:52
  591.0 10.5 multiply_reduce_fusion.12
  601.5 122.2 %psum.138 = f32[2]{0:T(128)S(1)} all-reduce(f32[2]{0:T(128)S(1)} %get-tuple-element.50), channel_id=1, replica_groups=mesh['sub'=64,'rhs'=4] {'sub'}, use_global_device_ids=true, to_apply=%region_11.14 | all-reduce | flops 2 | bytes 16 | tf_op jit(solution)/shard_map/psum | solution.py:79
  729.8 125.9 %psum.139 = f32[2]{0:T(128)S(1)} all-reduce(f32[2]{0:T(128)S(1)} %get-tuple-element.52), channel_id=1, replica_groups=mesh['sub'=64,'rhs'=4] {'sub'}, use_global_device_ids=true, to_apply=%region_13.16 | all-reduce | flops 2 | bytes 16 | tf_op jit(solution)/shard_map/psum | solution.py:52
  864.3 11.1 multiply_reduce_fusion.1
  875.5 122.0 %all-reduce.3 = (f32[2]{0:T(128)S(1)}, f32[2]{0:T(128)S(1)}) all-reduce(f32[2]{0:T(128)S(1)} %get-tuple-element.6, f32[2]{0:T(128)S(1)} %get-tuple-element.5), channel_id=1, replica_groups=mesh['sub'=64,'rhs'=4] {'sub'}, use_global_device_ids=true, to_apply=%region_15.18 | all-reduce | flops 4 | bytes 32 | tf_op jit(solution)/shard_map/psum | solution.py:79
  1000.7 4.2 collective-permute-start.9
  1006.6 10.5 multiply_reduce_fusion.8
  1017.1 123.4 %psum.142 = f32[2]{0:T(128)S(1)} all-reduce(f32[2]{0:T(128)S(1)} %get-tuple-element.55), channel_id=1, replica_groups=mesh['sub'=64,'rhs'=4] {'sub'}, use_global_device_ids=true, to_apply=%region_19.22 | all-reduce | flops 2 | bytes 16 | tf_op jit(solution)/shard_map/psum | solution.py:100
  1146.6 5.2 fusion.64
  1151.9 124.5 %all-reduce.2 = (f32[2]{0:T(128)S(1)}, f32[2]{0:T(128)S(1)}) all-reduce(f32[2]{0:T(128)S(1)} %copy-done.43, f32[2]{0:T(128)S(1)} %get-tuple-element.57), channel_id=1, replica_groups=mesh['sub'=64,'rhs'=4] {'sub'}, use_global_device_ids=true, to_apply=%region_21.24 | all-reduce | flops 4 | bytes 32 | tf_op jit(solution)/shard_map/psum | solution.py:100
  1282.2 5.4 fusion.63
  1288.6 10.5 multiply_reduce_fusion.5
  1299.1 123.0 %psum.145 = f32[2]{0:T(128)S(1)} all-reduce(f32[2]{0:T(128)S(1)} %get-tuple-element.59), channel_id=1, replica_groups=mesh['sub'=64,'rhs'=4] {'sub'}, use_global_device_ids=true, to_apply=%region_25.28 | all-reduce | flops 2 | bytes 16 | tf_op jit(solution)/shard_map/psum | solution.py:100
  1428.2 5.2 fusion.66
  1433.5 125.2 %all-reduce.1 = (f32[2]{0:T(128)S(1)}, f32[2]{0:T(128)S(1)}) all-reduce(f32[2]{0:T(128)S(1)} %copy-done.42, f32[2]{0:T(128)S(1)} %get-tuple-element.61), channel_id=1, replica_groups=mesh['sub'=64,'rhs'=4] {'sub'}, use_global_device_ids=true, to_apply=%region_27.30 | all-reduce | flops 4 | bytes 32 | tf_op jit(solution)/shard_map/psum | solution.py:100
  1564.0 5.3 fusion.65
  1570.2 10.5 multiply_reduce_fusion.2
  1580.7 123.3 %psum.148 = f32[2]{0:T(128)S(1)} all-reduce(f32[2]{0:T(128)S(1)} %get-tuple-element.63), channel_id=1, replica_groups=mesh['sub'=64,'rhs'=4] {'sub'}, use_global_device_ids=true, to_apply=%region_31.34 | all-reduce | flops 2 | bytes 16 | tf_op jit(solution)/shard_map/psum | solution.py:100
  1710.1 5.2 fusion.68
  1715.4 125.2 %all-reduce = (f32[2]{0:T(128)S(1)}, f32[2]{0:T(128)S(1)}) all-reduce(f32[2]{0:T(128)S(1)} %copy-done.41, f32[2]{0:T(128)S(1)} %get-tuple-element.65), channel_id=1, replica_groups=mesh['sub'=64,'rhs'=4] {'sub'}, use_global_device_ids=true, to_apply=%region_33.36 | all-reduce | flops 4 | bytes 32 | tf_op jit(solution)/shard_map/psum | solution.py:100
  1845.9 5.3 fusion.67
  1852.1 10.8 fusion.1
  1870.6 4.3 add_add_fusion
  1878.2 106.4 %all-reduce.7.cloned.1.call-done = f32[48,9216]{1,0:T(8,128)} async-done(((f32[48,9216]{1,0:T(8,128)}), f32[48,9216]{1,0:T(8,128)}) %all-reduce.7.cloned.1.call-update) | async-done | bytes 1769488 | tf_op jit(solution)/shard_map/psum | solution.py:125
  (224 shorter events, 114.0 us)
Async XLA Ops:
  7.2 1977.4 %all-reduce.7.cloned.1.call-start = ((), (), s32[]{:S(2)}) async-start(), calls=%async_computation | async-start | bytes 3538944 | tf_op jit(solution)/shard_map/psum | solution.py:125
  18.9 17.5 collective-permute-start
  23.5 12.9 collective-permute-start.1
  179.5 148.7 %copy-start.6 = (f32[2,48,96]{2,0,1:T(2,128)}, f32[2,48,96]{2,0,1:T(2,128)S(1)}, u32[]{:S(2)}) copy-start(f32[2,48,96]{2,0,1:T(2,128)S(1)} %convolution_bitcast_fusion.20) | copy-start | bytes 110596
  309.9 4.3 collective-permute-start.2
  311.8 4.9 collective-permute-start.3
  583.2 4.3 collective-permute-start.4
  585.1 4.9 collective-permute-start.5
  723.8 137.1 %copy-start.12 = (f32[2,4608]{1,0:T(2,128)S(1)}, f32[2,4608]{1,0:T(2,128)}, u32[]{:S(2)}) copy-start(f32[2,4608]{1,0:T(2,128)} %param.14) | copy-start | bytes 110596
  855.8 141.7 %copy-start.27 = (f32[2]{0:T(128)}, f32[2]{0:T(128)S(1)}, u32[]{:S(2)}) copy-start(f32[2]{0:T(128)S(1)} %psum.139) | copy-start | bytes 28
  856.5 4.5 collective-permute-start.6
  858.5 4.9 collective-permute-start.7
  998.8 6.2 collective-permute-start.8
  1000.7 4.9 collective-permute-start.9
  1006.6 134.0 %copy-start.38 = (f32[2]{0:T(128)S(1)}, f32[2]{0:T(128)}, u32[]{:S(2)}) copy-start(f32[2]{0:T(128)} %copy-done.37) | copy-start | bytes 28
  1006.6 133.9 %copy-start.40 = (f32[2]{0:T(128)S(1)}, f32[2]{0:T(128)}, u32[]{:S(2)}) copy-start(f32[2]{0:T(128)} %copy-done.39) | copy-start | bytes 28
  1144.4 137.8 %copy-start.11 = (f32[2,48,96]{2,0,1:T(2,128)S(1)}, f32[2,48,96]{2,0,1:T(2,128)}, u32[]{:S(2)}) copy-start(f32[2,48,96]{2,0,1:T(2,128)} %copy-done.10) | copy-start | bytes 110596
  1277.7 9.9 collective-permute-start.10
  1279.7 8.0 collective-permute-start.11
  1288.5 133.6 %copy-start.26 = (f32[2]{0:T(128)S(1)}, f32[2]{0:T(128)}, u32[]{:S(2)}) copy-start(f32[2]{0:T(128)} %copy-done.24) | copy-start | bytes 28
  1288.5 133.6 %copy-start.28 = (f32[2]{0:T(128)S(1)}, f32[2]{0:T(128)}, u32[]{:S(2)}) copy-start(f32[2]{0:T(128)} %copy-done.27) | copy-start | bytes 28
  1426.0 138.0 %copy-start.9 = (f32[2,48,96]{2,0,1:T(2,128)S(1)}, f32[2,48,96]{2,0,1:T(2,128)}, u32[]{:S(2)}) copy-start(f32[2,48,96]{2,0,1:T(2,128)} %copy-done.8) | copy-start | bytes 110596
  1428.2 142.0 %copy-start.17 = (f32[2]{0:T(128)S(1)}, f32[2]{0:T(128)}, u32[]{:S(2)}) copy-start(f32[2]{0:T(128)} %copy-done.16) | copy-start | bytes 28
  1559.4 9.9 collective-permute-start.12
  1561.3 8.0 collective-permute-start.13
  1570.2 133.8 %copy-start.20 = (f32[2]{0:T(128)S(1)}, f32[2]{0:T(128)}, u32[]{:S(2)}) copy-start(f32[2]{0:T(128)} %copy-done.19) | copy-start | bytes 28
  1570.2 133.8 %copy-start.23 = (f32[2]{0:T(128)S(1)}, f32[2]{0:T(128)}, u32[]{:S(2)}) copy-start(f32[2]{0:T(128)} %copy-done.21) | copy-start | bytes 28
  1570.2 133.8 %copy-start.30 = (f32[2]{0:T(128)S(1)}, f32[2]{0:T(128)}, u32[]{:S(2)}) copy-start(f32[2]{0:T(128)} %copy-done.29) | copy-start | bytes 28
  1707.9 138.0 %copy-start.7 = (f32[2,48,96]{2,0,1:T(2,128)S(1)}, f32[2,48,96]{2,0,1:T(2,128)}, u32[]{:S(2)}) copy-start(f32[2,48,96]{2,0,1:T(2,128)} %copy-done.6) | copy-start | bytes 110596
  1710.1 142.0 %copy-start.15 = (f32[2]{0:T(128)S(1)}, f32[2]{0:T(128)}, u32[]{:S(2)}) copy-start(f32[2]{0:T(128)} %copy-done.14) | copy-start | bytes 28
  1841.3 9.8 collective-permute-start.14
  1843.3 7.9 collective-permute-start.15
  (31 other events, 1385.0 us)
Sparse Core Ops, SparseCore 0:
  1877.6 106.9 all-reduce.6
where the time goes:
time: 2000 us; the launch traced here: 1990 us
  blocking collectives  1620 us (81%)
  matrix products  170 us (8%)
  waiting for transfers between devices  115 us (6%)
  starting transfers between devices  39.2 us (2%)
  local copies, waits for them, and re-layouts  32.9 us (2%)
    psum x6, blocking collectives, shards(): lax.psum((local_dot(dir_bar, direction), local_dot(target, direction)), '...  745 us
    psum x4, blocking collectives, norm_sum(): return lax.psum(local_dot(first_vec, second_vec), 'sub')  507 us
    psum x3, blocking collectives, shards(): curvature = lax.psum(local_dot(direction, applied), 'sub')  366 us
    psum x1, waiting for transfers between devices, shards(): grad_sum = lax.psum(grad_sum, 'rhs')  106 us
    dot_general x8, matrix products, block_product(): return jnp.einsum('nkab,rnkb->rna', blocks, gathered, precision=highest)  84.9 us
  transfers between devices with their start and end apart: 17, of which 5 were waited for; matrix products, arithmetic and copies ran while one was open for 1% of the time, Pallas kernels for 0%

commit v1 on v0

--- a/solution.py
+++ b/solution.py
@@ -49,7 +49,7 @@
 
 
 def norm_sum(first_vec, second_vec):
-    return lax.psum(local_dot(first_vec, second_vec), "sub")
+    return jnp.sum(lax.all_gather(local_dot(first_vec, second_vec), "sub"), axis=0)
 
 
 def grad_term(projected, zeta_bar, weight_zeta, resid_vec):

time: 2000 us -> 2010 us (level)
    psum x4 -> x0, blocking collectives: 507 us -> none  [norm_sum(): return lax.psum(local_dot(first_vec, second_vec), 'sub')]
    unnamed x0 -> x4, blocking collectives: none -> 507 us
where the time goes in v1:
time: 2010 us; the launch traced here: 2000 us
  blocking collectives  1620 us (81%)
  matrix products  170 us (8%)
  waiting for transfers between devices  115 us (6%)
  starting transfers between devices  39.2 us (2%)
  local copies, waits for them, and re-layouts  36.5 us (2%)
    psum x6, blocking collectives, shards(): lax.psum((local_dot(dir_bar, direction), local_dot(target, direction)), '...  745 us
    unnamed x4, blocking collectives  507 us
    psum x3, blocking collectives, shards(): curvature = lax.psum(local_dot(direction, applied), 'sub')  366 us
    psum x1, waiting for transfers between devices, shards(): grad_sum = lax.psum(grad_sum, 'rhs')  106 us
    dot_general x8, matrix products, block_product(): return jnp.einsum('nkab,rnkb->rna', blocks, gathered, precision=highest)  84.9 us
  transfers between devices with their start and end apart: 17, of which 5 were waited for; matrix products, arithmetic and copies ran while one was open for 1% of the time, Pallas kernels for 0%

profile of v1, /device:TPU:1, one launch (start us, length us, event | category | flops | bytes accessed | tf_op | source)
XLA Modules:
  0.0 1998.8 jit_solution(3692403261892643792)
XLA Ops:
  18.9 4.6 collective-permute-start
  25.8 10.6 reshape.66
  38.6 10.5 multiply_reduce_fusion.16
  49.4 127.8 %all-reduce.8 = (f32[128]{0:T(128)S(1)}, f32[2]{0:T(128)S(1)}) all-reduce(f32[128]{0:T(128)S(1)} %dynamic-update-slice, f32[2]{0:T(128)S(1)} %get-tuple-element.9), channel_id=2, replica_groups=mesh['sub'=64,'rhs'=4] {'sub'}, use_global_device_ids=true, to_apply=%add | all-reduce | flops 130 | bytes 1040
  183.7 127.3 %all-reduce.1 = f32[128]{0:T(128)S(1)} all-reduce(f32[128]{0:T(128)S(1)} %dynamic-update-slice.1), channel_id=3, replica_groups=mesh['sub'=64,'rhs'=4] {'sub'}, use_global_device_ids=true, to_apply=%add.1 | all-reduce | flops 128 | bytes 1024
  319.8 10.5 multiply_reduce_fusion.14
  330.3 122.2 %psum.106 = f32[2]{0:T(128)S(1)} all-reduce(f32[2]{0:T(128)S(1)} %get-tuple-element.46), channel_id=1, replica_groups=mesh['sub'=64,'rhs'=4] {'sub'}, use_global_device_ids=true, to_apply=%region_7.10 | all-reduce | flops 2 | bytes 16 | tf_op jit(solution)/shard_map/psum | solution.py:79
  458.8 125.9 %all-reduce.2 = f32[128]{0:T(128)S(1)} all-reduce(f32[128]{0:T(128)S(1)} %dynamic-update-slice.2), channel_id=4, replica_groups=mesh['sub'=64,'rhs'=4] {'sub'}, use_global_device_ids=true, to_apply=%add.2 | all-reduce | flops 128 | bytes 1024
  593.5 10.5 multiply_reduce_fusion.12
  604.0 122.2 %psum.107 = f32[2]{0:T(128)S(1)} all-reduce(f32[2]{0:T(128)S(1)} %get-tuple-element.50), channel_id=1, replica_groups=mesh['sub'=64,'rhs'=4] {'sub'}, use_global_device_ids=true, to_apply=%region_11.14 | all-reduce | flops 2 | bytes 16 | tf_op jit(solution)/shard_map/psum | solution.py:79
  733.1 125.9 %all-reduce.3 = f32[128]{0:T(128)S(1)} all-reduce(f32[128]{0:T(128)S(1)} %dynamic-update-slice.3), channel_id=5, replica_groups=mesh['sub'=64,'rhs'=4] {'sub'}, use_global_device_ids=true, to_apply=%add.3 | all-reduce | flops 128 | bytes 1024
  867.8 11.1 multiply_reduce_fusion.1
  878.9 122.0 %all-reduce.7 = (f32[2]{0:T(128)S(1)}, f32[2]{0:T(128)S(1)}) all-reduce(f32[2]{0:T(128)S(1)} %get-tuple-element.6, f32[2]{0:T(128)S(1)} %get-tuple-element.5), channel_id=1, replica_groups=mesh['sub'=64,'rhs'=4] {'sub'}, use_global_device_ids=true, to_apply=%region_15.18 | all-reduce | flops 4 | bytes 32 | tf_op jit(solution)/shard_map/psum | solution.py:79
  1004.1 4.2 collective-permute-start.9
  1010.0 10.5 multiply_reduce_fusion.8
  1020.5 123.4 %psum.110 = f32[2]{0:T(128)S(1)} all-reduce(f32[2]{0:T(128)S(1)} %get-tuple-element.55), channel_id=1, replica_groups=mesh['sub'=64,'rhs'=4] {'sub'}, use_global_device_ids=true, to_apply=%region_19.22 | all-reduce | flops 2 | bytes 16 | tf_op jit(solution)/shard_map/psum | solution.py:100
  1150.5 5.2 fusion.64
  1155.8 124.5 %all-reduce.6 = (f32[2]{0:T(128)S(1)}, f32[2]{0:T(128)S(1)}) all-reduce(f32[2]{0:T(128)S(1)} %copy-done.42, f32[2]{0:T(128)S(1)} %get-tuple-element.57), channel_id=1, replica_groups=mesh['sub'=64,'rhs'=4] {'sub'}, use_global_device_ids=true, to_apply=%region_21.24 | all-reduce | flops 4 | bytes 32 | tf_op jit(solution)/shard_map/psum | solution.py:100
  1286.1 5.4 fusion.63
  1292.4 10.5 multiply_reduce_fusion.5
  1303.0 123.0 %psum.113 = f32[2]{0:T(128)S(1)} all-reduce(f32[2]{0:T(128)S(1)} %get-tuple-element.59), channel_id=1, replica_groups=mesh['sub'=64,'rhs'=4] {'sub'}, use_global_device_ids=true, to_apply=%region_25.28 | all-reduce | flops 2 | bytes 16 | tf_op jit(solution)/shard_map/psum | solution.py:100
  1432.6 5.2 fusion.66
  1437.8 125.2 %all-reduce.5 = (f32[2]{0:T(128)S(1)}, f32[2]{0:T(128)S(1)}) all-reduce(f32[2]{0:T(128)S(1)} %copy-done.41, f32[2]{0:T(128)S(1)} %get-tuple-element.61), channel_id=1, replica_groups=mesh['sub'=64,'rhs'=4] {'sub'}, use_global_device_ids=true, to_apply=%region_27.30 | all-reduce | flops 4 | bytes 32 | tf_op jit(solution)/shard_map/psum | solution.py:100
  1568.4 5.3 fusion.65
  1574.6 10.5 multiply_reduce_fusion.2
  1585.1 123.3 %psum.116 = f32[2]{0:T(128)S(1)} all-reduce(f32[2]{0:T(128)S(1)} %get-tuple-element.63), channel_id=1, replica_groups=mesh['sub'=64,'rhs'=4] {'sub'}, use_global_device_ids=true, to_apply=%region_31.34 | all-reduce | flops 2 | bytes 16 | tf_op jit(solution)/shard_map/psum | solution.py:100
  1714.5 5.2 fusion.68
  1719.7 125.2 %all-reduce.4 = (f32[2]{0:T(128)S(1)}, f32[2]{0:T(128)S(1)}) all-reduce(f32[2]{0:T(128)S(1)} %copy-done.40, f32[2]{0:T(128)S(1)} %get-tuple-element.65), channel_id=1, replica_groups=mesh['sub'=64,'rhs'=4] {'sub'}, use_global_device_ids=true, to_apply=%region_33.36 | all-reduce | flops 4 | bytes 32 | tf_op jit(solution)/shard_map/psum | solution.py:100
  1850.2 5.3 fusion.67
  1856.5 10.8 fusion.1
  1874.9 4.3 add_add_fusion
  1882.6 106.4 %all-reduce.11.cloned.1.call-done = f32[48,9216]{1,0:T(8,128)} async-done(((f32[48,9216]{1,0:T(8,128)}), f32[48,9216]{1,0:T(8,128)}) %all-reduce.11.cloned.1.call-update) | async-done | bytes 1769488 | tf_op jit(solution)/shard_map/psum | solution.py:125
  (241 shorter events, 117.6 us)
Async XLA Ops:
  7.2 1981.8 %all-reduce.11.cloned.1.call-start = ((), (), s32[]{:S(2)}) async-start(), calls=%async_computation | async-start | bytes 3538944 | tf_op jit(solution)/shard_map/psum | solution.py:125
  18.9 18.7 collective-permute-start
  23.5 14.1 collective-permute-start.1
  177.3 133.9 %copy-start.14 = (f32[2]{0:T(128)}, f32[2]{0:T(128)S(1)}, u32[]{:S(2)}) copy-start(f32[2]{0:T(128)S(1)} %reduce_sum.199) | copy-start | bytes 28
  181.2 149.1 %copy-start.6 = (f32[2,48,96]{2,0,1:T(2,128)}, f32[2,48,96]{2,0,1:T(2,128)S(1)}, u32[]{:S(2)}) copy-start(f32[2,48,96]{2,0,1:T(2,128)S(1)} %convolution_bitcast_fusion.20) | copy-start | bytes 110596
  312.0 4.3 collective-permute-start.2
  313.9 4.9 collective-permute-start.3
  585.7 4.3 collective-permute-start.4
  587.6 4.9 collective-permute-start.5
  726.8 137.5 %copy-start.12 = (f32[2,4608]{1,0:T(2,128)S(1)}, f32[2,4608]{1,0:T(2,128)}, u32[]{:S(2)}) copy-start(f32[2,4608]{1,0:T(2,128)} %param.14) | copy-start | bytes 110596
  859.2 141.7 %copy-start.16 = (f32[2]{0:T(128)}, f32[2]{0:T(128)S(1)}, u32[]{:S(2)}) copy-start(f32[2]{0:T(128)S(1)} %reduce_sum.208) | copy-start | bytes 28
  860.0 4.5 collective-permute-start.6
  861.9 4.9 collective-permute-start.7
  1002.2 6.2 collective-permute-start.8
  1004.1 4.9 collective-permute-start.9
  1010.0 134.0 %copy-start.37 = (f32[2]{0:T(128)S(1)}, f32[2]{0:T(128)}, u32[]{:S(2)}) copy-start(f32[2]{0:T(128)} %copy-done.36) | copy-start | bytes 28
  1010.0 133.9 %copy-start.39 = (f32[2]{0:T(128)S(1)}, f32[2]{0:T(128)}, u32[]{:S(2)}) copy-start(f32[2]{0:T(128)} %copy-done.38) | copy-start | bytes 28
  1148.3 137.8 %copy-start.11 = (f32[2,48,96]{2,0,1:T(2,128)S(1)}, f32[2,48,96]{2,0,1:T(2,128)}, u32[]{:S(2)}) copy-start(f32[2,48,96]{2,0,1:T(2,128)} %copy-done.10) | copy-start | bytes 110596
  1281.6 9.9 collective-permute-start.10
  1283.5 8.0 collective-permute-start.11
  1292.4 133.6 %copy-start.17 = (f32[2]{0:T(128)S(1)}, f32[2]{0:T(128)}, u32[]{:S(2)}) copy-start(f32[2]{0:T(128)} %copy-done.16) | copy-start | bytes 28
  1292.4 133.6 %copy-start.27 = (f32[2]{0:T(128)S(1)}, f32[2]{0:T(128)}, u32[]{:S(2)}) copy-start(f32[2]{0:T(128)} %copy-done.25) | copy-start | bytes 28
  1430.4 138.0 %copy-start.9 = (f32[2,48,96]{2,0,1:T(2,128)S(1)}, f32[2,48,96]{2,0,1:T(2,128)}, u32[]{:S(2)}) copy-start(f32[2,48,96]{2,0,1:T(2,128)} %copy-done.8) | copy-start | bytes 110596
  1432.6 142.0 %copy-start.21 = (f32[2]{0:T(128)S(1)}, f32[2]{0:T(128)}, u32[]{:S(2)}) copy-start(f32[2]{0:T(128)} %copy-done.20) | copy-start | bytes 28
  1563.8 9.9 collective-permute-start.12
  1565.7 8.0 collective-permute-start.13
  1574.6 133.8 %copy-start.15 = (f32[2]{0:T(128)S(1)}, f32[2]{0:T(128)}, u32[]{:S(2)}) copy-start(f32[2]{0:T(128)} %copy-done.14) | copy-start | bytes 28
  1574.6 133.8 %copy-start.29 = (f32[2]{0:T(128)S(1)}, f32[2]{0:T(128)}, u32[]{:S(2)}) copy-start(f32[2]{0:T(128)} %copy-done.28) | copy-start | bytes 28
  1712.2 138.0 %copy-start.7 = (f32[2,48,96]{2,0,1:T(2,128)S(1)}, f32[2,48,96]{2,0,1:T(2,128)}, u32[]{:S(2)}) copy-start(f32[2,48,96]{2,0,1:T(2,128)} %copy-done.6) | copy-start | bytes 110596
  1714.5 142.0 %copy-start.19 = (f32[2]{0:T(128)S(1)}, f32[2]{0:T(128)}, u32[]{:S(2)}) copy-start(f32[2]{0:T(128)} %copy-done.18) | copy-start | bytes 28
  1845.7 9.8 collective-permute-start.14
  1847.6 7.9 collective-permute-start.15
  (31 other events, 1229.7 us)
Sparse Core Ops, SparseCore 0:
  1882.0 106.9 all-reduce.10
